TPU v7x, 256 devices: a whole 4x4x8 slice. The times are simulated.
256 devices in a mesh: seq: 16 (over y, z_hi), fsdp: 16 (over x, z_lo, core).
Axes of the slice: x: 4, y: 4, z: 8 (z_hi: 4, z_lo: 2; z = z_hi * 2 + z_lo), core: 2. Of those that a mesh axis runs over, the one named last changes fastest.
Arguments:
- tokens: bfloat16 [2048, 4096], P('seq', 'fsdp'), may hold values from -6 to 6
- in_weight: bfloat16 [3, 4096, 4096], P(None, 'seq', 'fsdp'), may hold values from -0.09375 to 0.09375
- out_weight: bfloat16 [4096, 4096], P('fsdp', 'seq'), may hold values from -0.09375 to 0.09375
- filters: float32 [4096, 128], P('fsdp'), may hold values from -0.5 to 0.5
- cotangent: bfloat16 [2048, 4096], P('seq', 'fsdp'), may hold values from -6 to 6
Outputs:
- mixed_out: bfloat16 [2048, 4096], P('seq', 'fsdp')
- grad_tokens: bfloat16 [2048, 4096], P('seq', 'fsdp')
- grad_in_weight: float32 [3, 4096, 4096], P(None, 'seq', 'fsdp')
- grad_out_weight: float32 [4096, 4096], P('fsdp', 'seq')
- grad_filters: float32 [4096, 128], P('fsdp')
All inputs are finite; a program needn't handle non-finite values.
Results may differ from a plain program's by a relative error of at most 0.018.
Values may be sent and summed in bfloat16 or wider, within the bound.
A program may use at most 64 MiB of HBM per device.

v0:
```python
import jax
import jax.numpy as jnp
from jax import lax
from jax.sharding import PartitionSpec as P

highest = lax.Precision.HIGHEST


def from_behind(value, axis, by):
    length = lax.axis_size(axis)
    pairs = [(i, i + by) for i in range(length) if 0 <= i + by < length]
    return lax.ppermute(value, axis, pairs)


def causal_filter(extended, filters):
    kernel = jnp.flip(jnp.transpose(filters), 0)[:, None, :]
    result = lax.conv_general_dilated(
        extended[None],
        kernel,
        (1,),
        "VALID",
        dimension_numbers=("NWC", "WIO", "NWC"),
        feature_group_count=filters.shape[0],
        precision=highest,
    )
    return result[0]


def reverse_filter(extended, filters):
    kernel = jnp.transpose(filters)[:, None, :]
    result = lax.conv_general_dilated(
        extended[None],
        kernel,
        (1,),
        "VALID",
        dimension_numbers=("NWC", "WIO", "NWC"),
        feature_group_count=filters.shape[0],
        precision=highest,
    )
    return result[0]


def filter_grad(extended, gradient):
    result = lax.conv_general_dilated(
        extended[None],
        gradient[:, None, :],
        (1,),
        "VALID",
        dimension_numbers=("NWC", "WIO", "NWC"),
        feature_group_count=gradient.shape[1],
        precision=highest,
    )
    return jnp.transpose(jnp.flip(result[0], 0))


def on_device(tokens, in_weight, out_weight, filters, cotangent):
    margin = filters.shape[1] - 1
    gathered = lax.all_gather(tokens, "fsdp", axis=1, tiled=True)
    out_full = lax.all_gather(out_weight, "seq", axis=1, tiled=True)
    in_full = lax.all_gather(in_weight, "seq", axis=1, tiled=True)
    projected = jnp.einsum("td,idc->itc", gathered, in_full, preferred_element_type=jnp.float32)
    projected = projected.astype(jnp.bfloat16)
    queries = projected[0].astype(jnp.float32)
    key_part = projected[1].astype(jnp.float32)
    value_part = projected[2].astype(jnp.float32)
    signal = (key_part * value_part).astype(jnp.bfloat16)
    earlier = from_behind(signal[-margin:], "seq", 1)
    extended = jnp.concatenate([earlier, signal], 0).astype(jnp.float32)
    filtered = causal_filter(extended, filters)
    gated_rows = (queries * filtered).astype(jnp.bfloat16)
    partial_value = jnp.dot(gated_rows, out_full, preferred_element_type=jnp.float32)
    mixed_out = lax.psum_scatter(
        partial_value.astype(jnp.bfloat16), "fsdp", scatter_dimension=1, tiled=True
    )
    grad_full = lax.all_gather(cotangent, "fsdp", axis=1, tiled=True)
    grad_gated = lax.dot_general(
        grad_full, out_full, (((1,), (1,)), ((), ())), preferred_element_type=jnp.float32
    )
    grad_queries = grad_gated * filtered
    grad_filtered = (grad_gated * queries).astype(jnp.bfloat16)
    later_rows = from_behind(grad_filtered[:margin], "seq", -1)
    grad_signal = reverse_filter(
        jnp.concatenate([grad_filtered, later_rows], 0).astype(jnp.float32), filters
    )
    grad_filters = lax.psum(
        filter_grad(extended, grad_filtered.astype(jnp.float32)).astype(jnp.bfloat16), "seq"
    ).astype(jnp.float32)
    grad_projected = jnp.stack(
        [grad_queries, grad_signal * value_part, grad_signal * key_part]
    ).astype(jnp.bfloat16)
    grad_partial = jnp.einsum(
        "itc,idc->td", grad_projected, in_full, preferred_element_type=jnp.float32
    )
    grad_tokens = lax.psum_scatter(
        grad_partial.astype(jnp.bfloat16), "fsdp", scatter_dimension=1, tiled=True
    )
    weight_in_part = jnp.einsum(
        "td,itc->idc", gathered, grad_projected, preferred_element_type=jnp.float32
    )
    weight_out_part = lax.dot_general(
        gated_rows, grad_full, (((0,), (0,)), ((), ())), preferred_element_type=jnp.float32
    )
    grad_in_weight, grad_out_weight = (
        lax.psum_scatter(
            weight_in_part.astype(jnp.bfloat16), "seq", scatter_dimension=1, tiled=True
        ).astype(jnp.float32),
        lax.psum_scatter(
            weight_out_part.astype(jnp.bfloat16), "seq", scatter_dimension=1, tiled=True
        ).astype(jnp.float32),
    )
    return (mixed_out, grad_tokens, grad_in_weight, grad_out_weight, grad_filters)


def solution(mesh):
    placed = (
        P("seq", "fsdp"),
        P(None, "seq", "fsdp"),
        P("fsdp", "seq"),
        P("fsdp", None),
        P("seq", "fsdp"),
    )
    return jax.shard_map(
        on_device,
        mesh=mesh,
        in_specs=placed,
        out_specs=(
            P("seq", "fsdp"),
            P("seq", "fsdp"),
            P(None, "seq", "fsdp"),
            P("fsdp", "seq"),
            P("fsdp", None),
        ),
        check_vma=False,
    )
```

profile of v0, /device:TPU:16, one launch (start us, length us, event | category | flops | bytes accessed | tf_op | source)
XLA Modules:
  0.0 766.9 jit_solution(3096591360201777987)
XLA Ops:
  10.0 38.7 %all-gather.7.cloned.1.call-done = bf16[128,4096]{1,0:T(8,128)(2,1)} async-done(((bf16[128,256]{1,0:T(8,128)(2,1)}), bf16[128,4096]{1,0:T(8,128)(2,1)}) %all-gather.7.cloned.1.call-update) | async-done | bytes 1048592 | tf_op jit(solution)/shard_map/all_gather | solution.py:58
  48.7 93.1 %all-gather.5.cloned.1.call-done = bf16[3,4096,256]{2,1,0:T(8,128)(2,1)} async-done(((bf16[3,256,256]{2,1,0:T(8,128)(2,1)}), bf16[3,4096,256]{2,1,0:T(8,128)(2,1)}) %all-gather.5.cloned.1.call-update) | async-done | bytes 6291472 | tf_op jit(solution)/shard_map/all_gather | solution.py:60
  141.8 4.1 fusion.2
  145.9 38.9 %all-gather.11.cloned.1.call-done = bf16[128,4096]{1,0:T(8,128)(2,1)} async-done(((bf16[128,256]{1,0:T(8,128)(2,1)}), bf16[128,4096]{1,0:T(8,128)(2,1)}) %all-gather.11.cloned.1.call-update) | async-done | bytes 1048592 | tf_op jit(solution)/shard_map/all_gather | solution.py:75
  184.8 64.7 %all-gather.9.cloned.1.call-done = bf16[256,4096]{1,0:T(8,128)(2,1)} async-done(((bf16[256,256]{1,0:T(8,128)(2,1)}), bf16[256,4096]{1,0:T(8,128)(2,1)}) %all-gather.9.cloned.1.call-update) | async-done | bytes 2097168 | tf_op jit(solution)/shard_map/all_gather | solution.py:59
  249.5 2.8 fusion.15
  252.3 3.5 collective-permute-start.1
  255.9 3.4 collective-permute-done.1
  260.8 3.8 collective-permute-start
  265.0 5.0 collective-permute-done
  270.0 1.4 fusion.9
  271.5 1.9 fusion.7
  274.1 2.0 convolution_convert_fusion.1
  276.3 4.4 fusion
  280.8 6.0 fusion.1
  286.9 1.5 convolution_convert_fusion.2
  288.4 137.5 %all-reduce.2.cloned.1.call-done = bf16[256,128]{0,1:T(8,128)(2,1)} async-done(((bf16[256,128]{0,1:T(8,128)(2,1)}), bf16[256,128]{0,1:T(8,128)(2,1)}) %all-reduce.2.cloned.1.call-update) | async-done | bytes 65552 | tf_op jit(solution)/shard_map/psum | solution.py:85
  425.9 1.6 copy.20
  427.5 87.5 %reduce-scatter.11.cloned.1.call-done = bf16[256,256]{1,0:T(8,128)(2,1)} async-done(((bf16[256,4096]{1,0:T(8,128)(2,1)}), bf16[256,256]{1,0:T(8,128)(2,1)}) %reduce-scatter.11.cloned.1.call-update) | async-done | bytes 131088 | tf_op jit(solution)/shard_map/reduce_scatter | solution.py:107
  515.1 1.6 convert_element_type.84
  516.7 110.3 %reduce-scatter.9.cloned.1.call-done = bf16[3,256,256]{1,2,0:T(8,128)(2,1)} async-done(((bf16[3,4096,256]{1,2,0:T(8,128)(2,1)}), bf16[3,256,256]{1,2,0:T(8,128)(2,1)}) %reduce-scatter.9.cloned.1.call-update) | async-done | bytes 393232 | tf_op jit(solution)/shard_map/reduce_scatter | solution.py:104
  627.0 2.0 copy.19
  629.0 65.3 %reduce-scatter.7.cloned.1.call-done = bf16[128,256]{1,0:T(8,128)(2,1)} async-done(((bf16[128,4096]{1,0:T(8,128)(2,1)}), bf16[128,256]{1,0:T(8,128)(2,1)}) %reduce-scatter.7.cloned.1.call-update) | async-done | bytes 65552 | tf_op jit(solution)/shard_map/reduce_scatter | solution.py:94
  694.3 66.1 %reduce-scatter.5.cloned.1.call-done = bf16[128,256]{1,0:T(8,128)(2,1)} async-done(((bf16[128,4096]{1,0:T(8,128)(2,1)}), bf16[128,256]{1,0:T(8,128)(2,1)}) %reduce-scatter.5.cloned.1.call-update) | async-done | bytes 65552 | tf_op jit(solution)/shard_map/reduce_scatter | solution.py:72
  (37 shorter events, 5.7 us)
Async XLA Ops:
  7.2 41.6 %all-gather.7.cloned.1.call-start = ((), (), s32[]{:S(2)}) async-start(), calls=%async_computation.5 | async-start | bytes 1114112 | tf_op jit(solution)/shard_map/all_gather | solution.py:58
  7.9 133.9 %all-gather.5.cloned.1.call-start = ((), (), s32[]{:S(2)}) async-start(), calls=%async_computation.4 | async-start | bytes 6684672 | tf_op jit(solution)/shard_map/all_gather | solution.py:60
  8.6 176.2 %all-gather.11.cloned.1.call-start = ((), (), s32[]{:S(2)}) async-start(), calls=%async_computation.8 | async-start | bytes 1114112 | tf_op jit(solution)/shard_map/all_gather | solution.py:75
  9.4 240.1 %all-gather.9.cloned.1.call-start = ((), (), s32[]{:S(2)}) async-start(), calls=%async_computation.6 | async-start | bytes 2228224 | tf_op jit(solution)/shard_map/all_gather | solution.py:59
  10.0 245.8 %copy-start.3 = (f32[256,128]{1,0:T(8,128)S(1)}, f32[256,128]{1,0:T(8,128)}, u32[]{:S(2)}) copy-start(f32[256,128]{1,0:T(8,128)} %param.8) | copy-start | bytes 393220
  10.0 416.0 %all-reduce.2.cloned.1.call-start = ((), (), s32[]{:S(2)}) async-start(), calls=%async_computation.12 | async-start | bytes 131072 | tf_op jit(solution)/shard_map/psum | solution.py:85
  252.3 7.1 collective-permute-start.1
  260.8 9.2 %collective-permute-start = (bf16[127,256]{1,0:T(8,128)(2,1)S(1)}, bf16[127,256]{1,0:T(8,128)(2,1)S(1)}, u32[]{:S(2)}, u32[]{:S(2)}) collective-permute-start(bf16[127,256]{1,0:T(8,128)(2,1)S(1)} %slice_bitcast_fusion), channel_id=1, source_target_pairs={{0,16},{16,32},{32,48},{48,64},{64,80},{80,96},{96,112},{112,128},... | collective-permute-start | bytes 195080 | tf_op jit(solution)/shard_map/ppermute | solution.py:12
  271.4 2.7 copy-start.2
  273.3 2.9 copy-start.1
  274.1 241.0 %reduce-scatter.11.cloned.1.call-start = ((), (), s32[]{:S(2)}) async-start(), calls=%async_computation.11 | async-start | bytes 2228224 | tf_op jit(solution)/shard_map/reduce_scatter | solution.py:107
  276.2 350.8 %reduce-scatter.9.cloned.1.call-start = ((), (), s32[]{:S(2)}) async-start(), calls=%async_computation.10 | async-start | bytes 6684672 | tf_op jit(solution)/shard_map/reduce_scatter | solution.py:104
  280.7 6.2 copy-start
  280.8 413.5 %reduce-scatter.7.cloned.1.call-start = ((), (), s32[]{:S(2)}) async-start(), calls=%async_computation.9 | async-start | bytes 1114112 | tf_op jit(solution)/shard_map/reduce_scatter | solution.py:94
  286.9 473.5 %reduce-scatter.5.cloned.1.call-start = ((), (), s32[]{:S(2)}) async-start(), calls=%async_computation.7 | async-start | bytes 1114112 | tf_op jit(solution)/shard_map/reduce_scatter | solution.py:72
Sparse Core Ops, SparseCore 0:
  9.7 38.9 all-gather.6
  51.2 90.5 all-gather.4
  143.6 41.1 all-gather.10
  187.1 62.4 all-gather.8
  274.2 151.6 all-reduce.1
  429.3 85.6 reduce-scatter.10
  518.8 108.1 reduce-scatter.8
  630.0 64.1 reduce-scatter.6
  697.4 62.9 reduce-scatter.4
where the time goes:
time: 767 us
  waiting for transfers between devices  713 us (93%)
  matrix products  25.5 us (3%)
  between operations  14 us (2%)
  starting transfers between devices  7.7 us (1%)
    psum x1, waiting for transfers between devices, on_device(): lax.psum(filter_grad(extended, grad_filtered.astype(jnp.float32)).astype(...  138 us
    reduce_scatter x1, waiting for transfers between devices, on_device(): lax.psum_scatter(weight_in_part.astype(jnp.bfloat16), 'seq', scatter_dime...  110 us
    all_gather x1, waiting for transfers between devices, on_device(): in_full = lax.all_gather(in_weight, 'seq', axis=1, tiled=True)  93.1 us
    reduce_scatter x1, waiting for transfers between devices, on_device(): lax.psum_scatter(weight_out_part.astype(jnp.bfloat16), 'seq', scatter_dim...  87.5 us
    reduce_scatter x1, waiting for transfers between devices, on_device(): lax.psum_scatter(partial_value.astype(jnp.bfloat16), 'fsdp', scatter_dime...  66.1 us
    reduce_scatter x1, waiting for transfers between devices, on_device(): lax.psum_scatter(grad_partial.astype(jnp.bfloat16), 'fsdp', scatter_dimen...  65.3 us
    all_gather x1, waiting for transfers between devices, on_device(): out_full = lax.all_gather(out_weight, 'seq', axis=1, tiled=True)  64.7 us
    all_gather x1, waiting for transfers between devices, on_device(): grad_full = lax.all_gather(cotangent, 'fsdp', axis=1, tiled=True)  38.9 us
  transfers between devices with their start and end apart: 11, of which 11 were waited for; matrix products, arithmetic and copies ran while one was open for 3% of the time, Pallas kernels for 0%

commit v1 on v0

--- a/solution.py
+++ b/solution.py
@@ -82,8 +82,11 @@
     grad_signal = reverse_filter(
         jnp.concatenate([grad_filtered, later_rows], 0).astype(jnp.float32), filters
     )
-    grad_filters = lax.psum(
-        filter_grad(extended, grad_filtered.astype(jnp.float32)).astype(jnp.bfloat16), "seq"
+    grad_filters = jnp.sum(
+        lax.all_gather(
+            filter_grad(extended, grad_filtered.astype(jnp.float32)).astype(jnp.bfloat16), "seq"
+        ),
+        axis=0,
     ).astype(jnp.float32)
     grad_projected = jnp.stack(
         [grad_queries, grad_signal * value_part, grad_signal * key_part]

time: 767 us -> 666 us (0.87)
  waiting for transfers between devices: 713 us -> 611 us
    psum x1 -> x0, waiting for transfers between devices: 138 us -> none  [on_device(): lax.psum(filter_grad(extended, grad_filtered.astype(jnp.float32)).astype(...]
    all_gather x0 -> x1, waiting for transfers between devices: none -> 34 us  [on_device(): lax.all_gather(filter_grad(extended, grad_filtered.astype(jnp.float32)).a...]
  transfers between devices with their start and end apart: 11 -> 11, of which waited for: 11 -> 11; matrix products, arithmetic and copies ran while one was open for 3% -> 4% of each run, Pallas kernels for 0% -> 0%
where the time goes in v1:
time: 666 us
  waiting for transfers between devices  611 us (92%)
  matrix products  25.6 us (4%)
  between operations  14 us (2%)
  starting transfers between devices  7.7 us (1%)
    reduce_scatter x1, waiting for transfers between devices, on_device(): lax.psum_scatter(weight_in_part.astype(jnp.bfloat16), 'seq', scatter_dime...  111 us
    all_gather x1, waiting for transfers between devices, on_device(): in_full = lax.all_gather(in_weight, 'seq', axis=1, tiled=True)  93.1 us
    reduce_scatter x1, waiting for transfers between devices, on_device(): lax.psum_scatter(weight_out_part.astype(jnp.bfloat16), 'seq', scatter_dim...  87.8 us
    reduce_scatter x1, waiting for transfers between devices, on_device(): lax.psum_scatter(partial_value.astype(jnp.bfloat16), 'fsdp', scatter_dime...  66.1 us
    reduce_scatter x1, waiting for transfers between devices, on_device(): lax.psum_scatter(grad_partial.astype(jnp.bfloat16), 'fsdp', scatter_dimen...  64.9 us
    all_gather x1, waiting for transfers between devices, on_device(): out_full = lax.all_gather(out_weight, 'seq', axis=1, tiled=True)  64.7 us
    all_gather x1, waiting for transfers between devices, on_device(): grad_full = lax.all_gather(cotangent, 'fsdp', axis=1, tiled=True)  38.9 us
    all_gather x1, waiting for transfers between devices, on_device(): gathered = lax.all_gather(tokens, 'fsdp', axis=1, tiled=True)  38.7 us
  transfers between devices with their start and end apart: 11, of which 11 were waited for; matrix products, arithmetic and copies ran while one was open for 4% of the time, Pallas kernels for 0%

profile of v1, /device:TPU:16, one launch (start us, length us, event | category | flops | bytes accessed | tf_op | source)
XLA Modules:
  0.0 665.6 jit_solution(15963377061991242508)
XLA Ops:
  10.0 38.7 %all-gather.9.cloned.1.call-done = bf16[128,4096]{1,0:T(8,128)(2,1)} async-done(((bf16[128,256]{1,0:T(8,128)(2,1)}), bf16[128,4096]{1,0:T(8,128)(2,1)}) %all-gather.9.cloned.1.call-update) | async-done | bytes 1048592 | tf_op jit(solution)/shard_map/all_gather | solution.py:58
  48.7 93.1 %all-gather.7.cloned.1.call-done = bf16[3,4096,256]{2,1,0:T(8,128)(2,1)} async-done(((bf16[3,256,256]{2,1,0:T(8,128)(2,1)}), bf16[3,4096,256]{2,1,0:T(8,128)(2,1)}) %all-gather.7.cloned.1.call-update) | async-done | bytes 6291472 | tf_op jit(solution)/shard_map/all_gather | solution.py:60
  141.8 4.1 fusion.2
  145.9 38.9 %all-gather.13.cloned.1.call-done = bf16[128,4096]{1,0:T(8,128)(2,1)} async-done(((bf16[128,256]{1,0:T(8,128)(2,1)}), bf16[128,4096]{1,0:T(8,128)(2,1)}) %all-gather.13.cloned.1.call-update) | async-done | bytes 1048592 | tf_op jit(solution)/shard_map/all_gather | solution.py:75
  184.8 64.7 %all-gather.11.cloned.1.call-done = bf16[256,4096]{1,0:T(8,128)(2,1)} async-done(((bf16[256,256]{1,0:T(8,128)(2,1)}), bf16[256,4096]{1,0:T(8,128)(2,1)}) %all-gather.11.cloned.1.call-update) | async-done | bytes 2097168 | tf_op jit(solution)/shard_map/all_gather | solution.py:59
  249.5 2.8 fusion.15
  252.3 3.5 collective-permute-start.1
  255.9 3.4 collective-permute-done.1
  260.8 3.8 collective-permute-start
  264.7 5.3 collective-permute-done
  270.0 1.9 fusion.7
  273.0 1.4 fusion.9
  274.4 2.0 convolution_convert_fusion.1
  276.6 4.4 fusion
  281.1 6.1 fusion.1
  287.3 1.5 convolution_convert_fusion.2
  288.8 34.0 %all-gather.15.cloned.1.call-done = bf16[4096,128]{0,1:T(8,128)(2,1)} async-done(((bf16[256,128]{0,1:T(8,128)(2,1)}), bf16[4096,128]{0,1:T(8,128)(2,1)}) %all-gather.15.cloned.1.call-update) | async-done | bytes 1048592 | tf_op jit(solution)/shard_map/all_gather | solution.py:86
  322.7 1.5 copy.34
  325.5 87.8 %reduce-scatter.11.cloned.1.call-done = bf16[256,256]{1,0:T(8,128)(2,1)} async-done(((bf16[256,4096]{1,0:T(8,128)(2,1)}), bf16[256,256]{1,0:T(8,128)(2,1)}) %reduce-scatter.11.cloned.1.call-update) | async-done | bytes 131088 | tf_op jit(solution)/shard_map/reduce_scatter | solution.py:110
  413.3 1.6 convert_element_type.86
  415.0 111.1 %reduce-scatter.9.cloned.1.call-done = bf16[3,256,256]{1,2,0:T(8,128)(2,1)} async-done(((bf16[3,4096,256]{1,2,0:T(8,128)(2,1)}), bf16[3,256,256]{1,2,0:T(8,128)(2,1)}) %reduce-scatter.9.cloned.1.call-update) | async-done | bytes 393232 | tf_op jit(solution)/shard_map/reduce_scatter | solution.py:107
  526.1 2.0 copy.29
  528.1 64.9 %reduce-scatter.7.cloned.1.call-done = bf16[128,256]{1,0:T(8,128)(2,1)} async-done(((bf16[128,4096]{1,0:T(8,128)(2,1)}), bf16[128,256]{1,0:T(8,128)(2,1)}) %reduce-scatter.7.cloned.1.call-update) | async-done | bytes 65552 | tf_op jit(solution)/shard_map/reduce_scatter | solution.py:97
  593.0 66.1 %reduce-scatter.5.cloned.1.call-done = bf16[128,256]{1,0:T(8,128)(2,1)} async-done(((bf16[128,4096]{1,0:T(8,128)(2,1)}), bf16[128,256]{1,0:T(8,128)(2,1)}) %reduce-scatter.5.cloned.1.call-update) | async-done | bytes 65552 | tf_op jit(solution)/shard_map/reduce_scatter | solution.py:72
  (39 shorter events, 7.0 us)
Async XLA Ops:
  7.2 41.6 %all-gather.9.cloned.1.call-start = ((), (), s32[]{:S(2)}) async-start(), calls=%async_computation.5 | async-start | bytes 1114112 | tf_op jit(solution)/shard_map/all_gather | solution.py:58
  7.9 133.9 %all-gather.7.cloned.1.call-start = ((), (), s32[]{:S(2)}) async-start(), calls=%async_computation.4 | async-start | bytes 6684672 | tf_op jit(solution)/shard_map/all_gather | solution.py:60
  8.6 176.2 %all-gather.13.cloned.1.call-start = ((), (), s32[]{:S(2)}) async-start(), calls=%async_computation.8 | async-start | bytes 1114112 | tf_op jit(solution)/shard_map/all_gather | solution.py:75
  9.4 240.1 %all-gather.11.cloned.1.call-start = ((), (), s32[]{:S(2)}) async-start(), calls=%async_computation.6 | async-start | bytes 2228224 | tf_op jit(solution)/shard_map/all_gather | solution.py:59
  10.0 245.8 %copy-start.3 = (f32[256,128]{1,0:T(8,128)S(1)}, f32[256,128]{1,0:T(8,128)}, u32[]{:S(2)}) copy-start(f32[256,128]{1,0:T(8,128)} %param.8) | copy-start | bytes 393220
  10.0 312.8 %all-gather.15.cloned.1.call-start = ((), (), s32[]{:S(2)}) async-start(), calls=%async_computation.12 | async-start | bytes 1114112 | tf_op jit(solution)/shard_map/all_gather | solution.py:86
  252.3 7.1 %collective-permute-start.1 = (bf16[127,256]{1,0:T(8,128)(2,1)S(1)}, bf16[127,256]{1,0:T(8,128)(2,1)S(1)}, u32[]{:S(2)}, u32[]{:S(2)}) collective-permute-start(bf16[127,256]{1,0:T(8,128)(2,1)S(1)} %bitcast.72), channel_id=1, source_target_pairs={{16,0},{32,16},{48,32},{64,48},{80,64},{96,80},{112,96},{128,112},... | collective-permute-start | bytes 195080 | tf_op jit(solution)/shard_map/ppermute | solution.py:12
  260.8 9.2 %collective-permute-start = (bf16[127,256]{1,0:T(8,128)(2,1)S(1)}, bf16[127,256]{1,0:T(8,128)(2,1)S(1)}, u32[]{:S(2)}, u32[]{:S(2)}) collective-permute-start(bf16[127,256]{1,0:T(8,128)(2,1)S(1)} %slice_bitcast_fusion), channel_id=1, source_target_pairs={{0,16},{16,32},{32,48},{48,64},{64,80},{80,96},{96,112},{112,128},... | collective-permute-start | bytes 195080 | tf_op jit(solution)/shard_map/ppermute | solution.py:12
  272.6 140.7 %reduce-scatter.11.cloned.1.call-start = ((), (), s32[]{:S(2)}) async-start(), calls=%async_computation.11 | async-start | bytes 2228224 | tf_op jit(solution)/shard_map/reduce_scatter | solution.py:110
  273.0 1.4 copy-start.2
  274.4 2.1 copy-start.1
  276.5 249.6 %reduce-scatter.9.cloned.1.call-start = ((), (), s32[]{:S(2)}) async-start(), calls=%async_computation.10 | async-start | bytes 6684672 | tf_op jit(solution)/shard_map/reduce_scatter | solution.py:107
  281.1 6.2 copy-start
  281.1 312.0 %reduce-scatter.7.cloned.1.call-start = ((), (), s32[]{:S(2)}) async-start(), calls=%async_computation.9 | async-start | bytes 1114112 | tf_op jit(solution)/shard_map/reduce_scatter | solution.py:97
  287.2 371.9 %reduce-scatter.5.cloned.1.call-start = ((), (), s32[]{:S(2)}) async-start(), calls=%async_computation.7 | async-start | bytes 1114112 | tf_op jit(solution)/shard_map/reduce_scatter | solution.py:72
Sparse Core Ops, SparseCore 0:
  9.7 38.9 all-gather.8
  51.2 90.5 all-gather.6
  143.6 41.1 all-gather.12
  187.1 62.4 all-gather.10
  272.8 49.9 all-gather.14
  326.2 87.1 reduce-scatter.10
  417.1 108.9 reduce-scatter.8
  529.2 63.8 reduce-scatter.6
  596.1 62.9 reduce-scatter.4
